TPU v7x, 512 devices: a whole 4x8x8 slice. The times are simulated.
512 devices in a mesh: grp: 4 (over x), dev: 128 (over z, y, core).
Axes of the slice: x: 4, y: 8, z: 8, core: 2. Of those that a mesh axis runs over, the one named last changes fastest.
Arguments:
- blocks: bfloat16 [4096, 64, 4096], P(('grp', 'dev')), may hold values from -6 to 6
- coords: int32 [3, 4096], P(None, ('grp', 'dev')), may hold values from 0 to 255, as said below
- counts: int32 [512], P(('grp', 'dev')), may hold values from 1 to 8, as said below
- row_place: int32 [256], replicated, may hold values from 0 to 255, as said below
- factor_one: bfloat16 [256, 4096], P('dev'), may hold values from -0.75 to 0.75
- factor_two: bfloat16 [256, 4096], P('dev'), may hold values from -0.75 to 0.75
- factor_three: bfloat16 [256, 4096], P('dev'), may hold values from -0.75 to 0.75
Outputs:
- new_rows: float32 [256, 4096], P('dev')
- gram: float32 [64, 64], replicated
Inputs may be any that keep to these rules, and one draw needn't show every extreme that they name: `coords`: every mode-1 id of a slot on the device with dev index d has its row-block position in [d * 2, (d + 1) * 2); on one device, the row-block positions of the mode-2 ids of its 8 slots lie in pairwise different ranges [e * 2, (e + 1) * 2), and so do those of the mode-3 ids. `counts`: some device has all 8 slots live. `row_place`: A permutation of 0 to 255.
All inputs are finite; a program needn't handle non-finite values.
Results may differ from a plain program's by a relative error of at most 0.0056.
Values may be sent and summed in bfloat16 or wider, within the bound.
A program may use at most 128 MiB of HBM per device.

v0:
```python
import jax
import jax.numpy as jnp
from jax import lax
from jax.sharding import PartitionSpec as P


def look_place(ids, row_place):
    table = jnp.arange(row_place.shape[0])
    hits = ids[:, None] == table[None, :]
    return jnp.sum(jnp.where(hits, row_place[None, :], 0), axis=1)


def body(blocks, coords, counts, row_place, factor_one, factor_two, factor_three):
    slot_count = blocks.shape[0]
    edge = blocks.shape[1]
    rank_width = factor_one.shape[1] // edge
    row_blocks = factor_one.shape[0]
    live = (jnp.arange(slot_count) < counts[0]).astype(jnp.float32)
    pos_one = look_place(coords[0], row_place)
    pos_two = look_place(coords[1], row_place)
    pos_three = look_place(coords[2], row_place)
    local_one = pos_one % row_blocks
    pieces = (
        lax.all_gather(factor_two, "dev", axis=0, tiled=True),
        lax.all_gather(factor_three, "dev", axis=0, tiled=True),
    )
    taken = pieces[0].shape[0]
    offsets = jnp.arange(taken)
    pick_two = (pos_two[:, None] == offsets[None, :]).astype(jnp.bfloat16)
    pick_three = (pos_three[:, None] == offsets[None, :]).astype(jnp.bfloat16)
    chosen_two = jnp.dot(pick_two, pieces[0], preferred_element_type=jnp.float32)
    chosen_three = jnp.dot(pick_three, pieces[1], preferred_element_type=jnp.float32)
    upper = chosen_two.astype(jnp.bfloat16).reshape(slot_count, edge, rank_width)
    lower = chosen_three.astype(jnp.bfloat16).reshape(slot_count, edge, rank_width)
    tensor_rows = blocks.reshape(slot_count, edge * edge, edge)
    first = jnp.einsum(
        "bmk,bks->bms", tensor_rows, lower, preferred_element_type=jnp.float32
    ).astype(jnp.bfloat16)
    first = first.reshape(slot_count, edge, edge, rank_width)
    contrib = jnp.einsum("bajs,bjr->bars", first, upper, preferred_element_type=jnp.float32)
    contrib = contrib.reshape(slot_count, edge, rank_width * rank_width)
    owners = jnp.arange(row_blocks)
    assign = (local_one[:, None] == owners[None, :]).astype(jnp.float32) * live[:, None]
    panels = jnp.einsum("bl,bam->lam", assign, contrib, precision=lax.Precision.HIGHEST)
    panels = panels.reshape(row_blocks * edge, rank_width * rank_width)
    old_rows = factor_one.reshape(row_blocks * edge, rank_width)
    summed = lax.psum(panels, "grp")
    panel_b = summed.astype(jnp.bfloat16)
    proj_terms = jnp.dot(panel_b.T, old_rows, preferred_element_type=jnp.float32)
    proj = lax.psum(proj_terms, "dev").astype(jnp.bfloat16)
    rows = jnp.dot(panel_b, proj, preferred_element_type=jnp.float32)
    gram_local = jnp.dot(
        rows.T, rows, precision=lax.Precision.HIGHEST, preferred_element_type=jnp.float32
    )
    gmat = lax.psum(gram_local, "dev")
    trace_value = jnp.trace(gmat)
    rows_total = row_blocks * edge * lax.axis_size("dev")
    new_rows = (rows * lax.rsqrt(trace_value / (rows_total * rank_width))).reshape(
        row_blocks, edge * rank_width
    )
    gram = gmat * (rank_width / trace_value)
    return (new_rows, gram)


def solution(mesh):
    placed = (
        P(("grp", "dev"), None, None),
        P(None, ("grp", "dev")),
        P(("grp", "dev")),
        P(),
        P("dev", None),
        P("dev", None),
        P("dev", None),
    )
    return jax.shard_map(
        body, mesh=mesh, in_specs=placed, out_specs=(P("dev", None), P()), check_vma=False
    )
```

profile of v0, /device:TPU:4, one launch (start us, length us, event | category | flops | bytes accessed | tf_op | source)
XLA Modules:
  0.0 1270.0 jit_solution(4635308471587969259)
XLA Ops:
  7.2 0.0 copy-start
  7.2 0.0 copy-start.1
  7.2 0.0 copy-start.2
  7.2 0.0 all-gather.7.cloned.1.call-start
  7.2 0.7 all-gather.7.cloned.1.call-update
  7.9 0.0 all-gather.5.cloned.1.call-start
  8.0 0.7 all-gather.5.cloned.1.call-update
  8.7 12.6 reshape.54
  21.9 0.0 copy-done
  21.9 0.1 reshape.58
  22.0 0.0 copy-done.1
  22.0 0.0 copy-done.2
  22.1 0.2 select_reduce_fusion.3
  22.3 76.6 %all-gather.7.cloned.1.call-done = bf16[128,2,4096]{2,1,0:T(2,128)(2,1)} async-done(((bf16[1,2,4096]{2,1,0:T(2,128)(2,1)}), bf16[128,2,4096]{2,1,0:T(2,128)(2,1)}) %all-gather.7.cloned.1.call-update) | async-done | bytes 2097168 | tf_op jit(solution)/shard_map/all_gather | solution.py:25
  98.9 2.7 reshape.63
  101.6 0.4 convolution_convert_fusion.1
  102.0 0.2 reshape.53
  102.2 8.4 fusion.2
  110.7 8.4 copy.40
  119.0 62.9 %all-gather.5.cloned.1.call-done = bf16[128,2,4096]{2,1,0:T(2,128)(2,1)} async-done(((bf16[1,2,4096]{2,1,0:T(2,128)(2,1)}), bf16[128,2,4096]{2,1,0:T(2,128)(2,1)}) %all-gather.5.cloned.1.call-update) | async-done | bytes 2097168 | tf_op jit(solution)/shard_map/all_gather | solution.py:24
  181.9 2.7 reshape.61
  184.7 0.4 convolution_convert_fusion.2
  185.1 0.2 reshape.52
  185.3 11.5 convolution_bitcast_fusion
  196.8 14.8 %reshape.56 = f32[8,64,4096]{2,1,0:T(8,128)} reshape(f32[8,64,64,64]{3,2,1,0:T(8,128)} %convolution_bitcast_fusion) | data formatting | bytes 16777216 | tf_op jit(solution)/shard_map/reshape | solution.py:41
  211.5 15.3 %fusion = f32[2,64,4096]{2,0,1:T(2,128)S(1)} fusion(f32[8,64,4096]{2,1,0:T(8,128)} %reshape.56, f32[8]{0:T(128)S(1)} %compare_convert_fusion, s32[8]{0:T(128)S(1)} %and_select_fusion), kind=kOutput, calls=%fused_computation.1 | convolution fusion | flops 50331680 | bytes 10485824 | tf_op jit(solution)/shard_map/bl,bam->lam/dot_general | solution.py:44
  226.8 1.2 copy.33
  228.1 42.2 %all-reduce.2 = bf16[128,4096]{1,0:T(8,128)(2,1)S(1)} all-reduce(f32[128,4096]{1,0:T(8,128)S(1)} %bitcast.38), channel_id=1, replica_groups=mesh['grp'=4,'dev'=128] {'grp'}, use_global_device_ids=true, to_apply=%region_3.4 | all-reduce | flops 524288 | bytes 3145728 | tf_op jit(solution)/shard_map/psum | solution.py:47
  270.2 0.3 fusion.21
  270.6 497.6 %all-reduce.3 = bf16[4096,64]{0,1:T(8,128)(2,1)S(1)} all-reduce(f32[4096,64]{0,1:T(8,128)S(1)} %fusion.21), channel_id=1, replica_groups=mesh['grp'=4,'dev'=128] {'dev'}, use_global_device_ids=true, to_apply=%region_4.5 | all-reduce | flops 262144 | bytes 1572864 | tf_op jit(solution)/shard_map/psum | solution.py:50
  768.2 0.5 fusion.20
  768.7 0.2 fusion.19
  768.9 490.9 %psum.23 = f32[64,64]{1,0:T(8,128)S(1)} all-reduce(f32[64,64]{1,0:T(8,128)S(1)} %fusion.19), channel_id=1, replica_groups=mesh['grp'=4,'dev'=128] {'dev'}, use_global_device_ids=true, to_apply=%region_5.6 | all-reduce | flops 4096 | bytes 32768 | tf_op jit(solution)/shard_map/psum | solution.py:55
  1259.7 0.6 select_reduce_fusion
  1261.0 0.6 broadcast_multiply_fusion
  1262.4 0.1 copy.34
  1262.4 0.7 reshape.59
  (4 shorter events, 0.0 us)
Async XLA Ops:
  7.2 14.7 %copy-start = (bf16[2,4096]{1,0:T(2,128)(2,1)S(1)}, bf16[2,4096]{1,0:T(2,128)(2,1)}, u32[]{:S(2)}) copy-start(bf16[2,4096]{1,0:T(2,128)(2,1)} %param.11) | copy-start | bytes 49156
  7.2 14.8 %copy-start.1 = (s32[3,8]{1,0:T(4,128)S(1)}, s32[3,8]{1,0:T(4,128)}, u32[]{:S(2)}) copy-start(s32[3,8]{1,0:T(4,128)} %param.8) | copy-start | bytes 292
  7.2 14.9 %copy-start.2 = (s32[256]{0:T(256)S(1)}, s32[256]{0:T(256)}, u32[]{:S(2)}) copy-start(s32[256]{0:T(256)} %param.10) | copy-start | bytes 3076
  7.2 91.7 %all-gather.7.cloned.1.call-start = ((), (), s32[]{:S(2)}) async-start(), calls=%async_computation.1 | async-start | bytes 2113536 | tf_op jit(solution)/shard_map/all_gather | solution.py:25
  7.9 174.0 %all-gather.5.cloned.1.call-start = ((), (), s32[]{:S(2)}) async-start(), calls=%async_computation | async-start | bytes 2113536 | tf_op jit(solution)/shard_map/all_gather | solution.py:24
Sparse Core Ops, SparseCore 0:
  11.1 87.6 all-gather.6
  102.0 79.9 all-gather.4
where the time goes:
time: 1270 us
  blocking collectives  1030 us (81%)
  waiting for transfers between devices  141 us (11%)
  local copies, waits for them, and re-layouts  43.7 us (3%)
  matrix products  37 us (3%)
  between operations  16.2 us (1%)
    psum x1, blocking collectives, body(): proj = lax.psum(proj_terms, 'dev').astype(jnp.bfloat16)  498 us
    psum x1, blocking collectives, body(): gmat = lax.psum(gram_local, 'dev')  491 us
    all_gather x1, waiting for transfers between devices, body(): lax.all_gather(factor_three, 'dev', axis=0, tiled=True)  76.6 us
    all_gather x1, waiting for transfers between devices, body(): lax.all_gather(factor_two, 'dev', axis=0, tiled=True)  62.9 us
    psum x1, blocking collectives, body(): summed = lax.psum(panels, 'grp')  42.2 us
  transfers between devices with their start and end apart: 2, of which 2 were waited for; matrix products, arithmetic and copies ran while one was open for 3% of the time, Pallas kernels for 0%

commit v1 on v0

v1 whole, which is shorter than its diff:
```python
import functools
import math

import jax
import jax.numpy as jnp
from jax import lax
from jax.experimental import pallas as pl
from jax.experimental.pallas import tpu as pltpu
from jax.sharding import PartitionSpec as P

MESH = pl.DeviceIdType.MESH
F32 = jnp.float32
BF16 = jnp.bfloat16
NT = (((1,), (1,)), ((), ()))


def place_of(n):
    d = lax.axis_index("dev")
    return lax.axis_index("grp"), d // (2 * n), (d // 2) % n, d % 2


def remote(src, dst, send, recv, target):
    copy = pltpu.make_async_remote_copy(
        src_ref=src, dst_ref=dst, send_sem=send, recv_sem=recv, device_id=target, device_id_type=MESH
    )
    copy.start()
    return copy


def look_place(ids, row_place):
    table = jnp.arange(row_place.shape[0])
    hits = ids[:, None] == table[None, :]
    return jnp.sum(jnp.where(hits, row_place[None, :], 0), axis=1)


def gather_kernel(n, two, three, out2, out3, own_sem, s1, r1, s2, r2, s3, r3):
    g, z, y, c = place_of(n)

    def dev(zz, yy, cc):
        return (g, (zz * n + yy) * 2 + cc)

    sibling = dev(z, y, 1 - c)
    barrier = pltpu.get_barrier_semaphore()
    for k in range(1, n):
        pl.semaphore_signal(barrier, inc=1, device_id=dev((z + k) % n, y, c), device_id_type=MESH)
        pl.semaphore_signal(barrier, inc=1, device_id=dev(z, (y + k) % n, c), device_id_type=MESH)
    pl.semaphore_signal(barrier, inc=1, device_id=sibling, device_id_type=MESH)
    own = [
        pltpu.make_async_copy(two, out2.at[z, y, c], own_sem.at[0]),
        pltpu.make_async_copy(three, out3.at[z, y, c], own_sem.at[1]),
    ]
    for copy in own:
        copy.start()
    pl.semaphore_wait(barrier, 2 * (n - 1) + 1)

    first = []
    for k in range(1, n):
        first.append(remote(two, out2.at[z, y, c], s1.at[0, k], r1.at[0, k], dev((z + k) % n, y, c)))
        first.append(remote(three, out3.at[z, y, c], s1.at[1, k], r1.at[1, k], dev(z, (y + k) % n, c)))
    for copy in own:
        copy.wait()
    for copy in first:
        copy.wait_recv()

    half = n // 2

    def bundle(which, at, part):
        lo, size = (0, n) if part is None else (part * half, half)
        if which == 0:
            return out2.at[pl.ds(lo, size), at, c]
        return out3.at[at, pl.ds(lo, size), c]

    def neighbour(which, step):
        if which == 0:
            return dev(z, (y + step + n) % n, c)
        return dev((z + step + n) % n, y, c)

    me = (y, z)
    sends, siblings = list(first), []

    def to_sibling(which, slot, at, part):
        ref = bundle(which, at, part)
        siblings.append(remote(ref, ref, s3.at[which, slot], r3.at[which, slot], sibling))

    rings = {}

    def pass_on(which, side, k, at):
        part = None if k < half else side
        ref = bundle(which, at, part)
        copy = remote(
            ref, ref, s2.at[which, side, k], r2.at[which, side, k], neighbour(which, 1 if side == 0 else -1)
        )
        rings[which, side, k] = copy
        sends.append(copy)

    for which in (0, 1):
        for side in (0, 1):
            pass_on(which, side, 1, me[which])
    for which in (0, 1):
        to_sibling(which, 0, me[which], None)
    for k in range(1, half + 1):
        for which in (0, 1):
            for side in (0, 1):
                rings[which, side, k].wait_recv()
                at = (me[which] + (n - k if side == 0 else k)) % n
                if k + 1 <= half:
                    pass_on(which, side, k + 1, at)
                to_sibling(which, 1 + 2 * (k - 1) + side, at, None if k < half else side)
    for copy in siblings:
        copy.wait_recv()
    for copy in sends + siblings:
        copy.wait_send()


def gather_factors(n, two, three):
    shape = jax.ShapeDtypeStruct((n, n, 2) + two.shape, two.dtype)
    dma = pltpu.SemaphoreType.DMA
    vmem = pl.BlockSpec(memory_space=pltpu.VMEM)
    return pl.pallas_call(
        functools.partial(gather_kernel, n),
        out_shape=(shape, shape),
        in_specs=[vmem] * 2,
        out_specs=(vmem, vmem),
        scratch_shapes=[
            dma((2,)),
            dma((2, n)),
            dma((2, n)),
            dma((2, 2, n)),
            dma((2, 2, n)),
            dma((2, n + 1)),
            dma((2, n + 1)),
        ],
        compiler_params=pltpu.CompilerParams(collective_id=0, has_side_effects=True),
        name="gather_factors",
    )(two, three)


def halves(v, odd):
    low = lax.broadcasted_iota(jnp.int32, v.shape, 1) < 64
    turned = pltpu.roll(v, 64, 1)
    left = jnp.where(low, v, turned)
    right = jnp.where(low, turned, v)
    return jnp.where(odd == 1, right, left)


def swap_pair(v0, v1):
    low = lax.broadcasted_iota(jnp.int32, v0.shape, 1) < 64
    even = jnp.where(low, v0, pltpu.roll(v1, 64, 1))
    odd = jnp.where(low, pltpu.roll(v0, 64, 1), v1)
    return even, odd


def local_kernel(info, blk, u2, u3, f1, panel, part, gs, xs, fs, uw, g2):
    s = pl.program_id(0)
    slots = pl.num_programs(0)
    for j in range(32):
        gs[j * 64 : (j + 1) * 64, :] = blk[0, :, j * 128 : (j + 1) * 128].astype(F32)
    for q in range(32):
        v0 = gs[pl.ds(2 * q, 32, stride=64), :]
        v1 = gs[pl.ds(2 * q + 1, 32, stride=64), :]
        even, odd = swap_pair(v0, v1)
        lanes = slice((q % 2) * 128, (q % 2) * 128 + 128)
        xs[q // 2, 0:32, lanes] = even.astype(BF16)
        xs[q // 2, 32:64, lanes] = odd.astype(BF16)

    lower = halves(u3[0].astype(F32), info[1, s] % 2)
    wide = jnp.concatenate([lower, lower], axis=1)
    wide = jnp.concatenate([wide] * 4, axis=0)
    rows = lax.broadcasted_iota(jnp.int32, wide.shape, 0) // 64
    cols = lax.broadcasted_iota(jnp.int32, wide.shape, 1) // 64
    wide = jnp.where(rows == cols, wide, 0.0).astype(BF16)
    first = jnp.dot(xs[...].reshape(1024, 256), wide, preferred_element_type=F32)
    start = pl.multiple_of(s * 64, 64)
    fs[:, pl.ds(start, 64), :] = first.astype(BF16).reshape(16, 64, 256)

    upper = halves(u2[0].astype(F32), info[0, s] % 2)
    owner = lax.broadcasted_iota(jnp.int32, upper.shape, 1) // 64
    keep = jnp.logical_and(owner == info[2, s], info[3, s] == 1)
    uw[pl.ds(start, 64), :] = jnp.where(keep, upper, 0.0).astype(BF16)

    @pl.when(s == slots - 1)
    def _():
        eye = (
            lax.broadcasted_iota(jnp.int32, (128, 128), 0) == lax.broadcasted_iota(jnp.int32, (128, 128), 1)
        ).astype(BF16)
        weights = lax.dot_general(eye, uw[...], NT, preferred_element_type=F32).astype(BF16)
        for q in range(16):
            out = jnp.dot(weights, fs[q], preferred_element_type=F32)
            g2[q * 256 : q * 256 + 128, :] = out[:, 0:128]
            g2[q * 256 + 128 : q * 256 + 256, :] = out[:, 128:256]
        for q in range(32):
            pair = []
            for r in (2 * q, 2 * q + 1):
                low = g2[pl.ds(r, 32, stride=128), :]
                high = g2[pl.ds(64 + r, 32, stride=128), :]
                pair.append(jnp.concatenate([low, high], axis=0))
            even, odd = swap_pair(*pair)
            lanes = slice((q % 2) * 128, (q % 2) * 128 + 128)
            panel[q // 2, 0:64, lanes] = even.astype(BF16)
            panel[q // 2, 64:128, lanes] = odd.astype(BF16)
        for q in range(16):
            part[q] = jnp.dot(f1[...], panel[q], preferred_element_type=F32)


def local_terms(info, blocks, two, three, f1):
    slots = blocks.shape[0]
    const2, const3 = (lambda s, i: (0, 0)), (lambda s, i: (0, 0, 0))
    return pl.pallas_call(
        local_kernel,
        grid_spec=pltpu.PrefetchScalarGridSpec(
            num_scalar_prefetch=1,
            grid=(slots,),
            in_specs=[
                pl.BlockSpec((1, 64, 4096), lambda s, i: (s, 0, 0)),
                pl.BlockSpec((1, 64, 128), lambda s, i: (i[0, s] // 2, 0, 0)),
                pl.BlockSpec((1, 64, 128), lambda s, i: (i[1, s] // 2, 0, 0)),
                pl.BlockSpec((64, 128), const2),
            ],
            out_specs=(pl.BlockSpec((16, 128, 256), const3), pl.BlockSpec((16, 64, 256), const3)),
            scratch_shapes=[
                pltpu.VMEM((2048, 128), F32),
                pltpu.VMEM((16, 64, 256), BF16),
                pltpu.VMEM((16, 64 * slots, 256), BF16),
                pltpu.VMEM((64 * slots, 128), BF16),
                pltpu.VMEM((4096, 128), F32),
            ],
        ),
        out_shape=(
            jax.ShapeDtypeStruct((16, 128, 256), BF16),
            jax.ShapeDtypeStruct((16, 64, 256), F32),
        ),
        compiler_params=pltpu.CompilerParams(dimension_semantics=("arbitrary",)),
        name="local_terms",
    )(info, blocks, two, three, f1)


def tail_kernel(
    n, nx, scale, panel, part, rows_out, gram_out,
    got_a, send_b, got_b, send_c, got_c, got_d, got_e, proj, row_t, got_h, gm, got_i, sum_i, got_j, sum_j, got_k,
    sa, ra, sb, rb, sc, rc, sd, rd, se, re, sf, rf, sg, rg, sh, rh, si, ri, sj, rj, sk, rk,
):
    g, z, y, c = place_of(n)

    def dev(zz, yy, cc):
        return (g, (zz * n + yy) * 2 + cc)

    def along_z(k):
        return dev((z + k) % n, y, c)

    def along_y(k):
        return dev(z, (y + k) % n, c)

    def along_x(k):
        return ((g + k) % nx, (z * n + y) * 2 + c)

    sibling = dev(z, y, 1 - c)
    barrier = pltpu.get_barrier_semaphore()
    for k in range(1, n):
        pl.semaphore_signal(barrier, inc=1, device_id=along_z(k), device_id_type=MESH)
        pl.semaphore_signal(barrier, inc=1, device_id=along_y(k), device_id_type=MESH)
    for k in range(1, nx):
        pl.semaphore_signal(barrier, inc=1, device_id=along_x(k), device_id_type=MESH)
    pl.semaphore_signal(barrier, inc=1, device_id=sibling, device_id_type=MESH)
    pl.semaphore_wait(barrier, 2 * (n - 1) + nx)

    gp = 8 // n
    tp = 8 * gp // n
    inner = (along_z, along_y)
    outer = (along_y, along_z)
    at_in = (z, y)
    at_out = (y, z)
    sends = []

    copy = remote(part.at[pl.ds((1 - c) * 8, 8)], got_a, sa, ra, sibling)
    sends.append(copy)
    copy.wait_recv()
    for q in range(8):
        both = part[c * 8 + q] + got_a[q]
        send_b[0, q] = both[0:32].astype(BF16)
        send_b[1, q] = both[32:64].astype(BF16)

    batch = []
    for k in range(1, n):
        for st in (0, 1):
            to = (at_in[st] + k) % n
            batch.append(remote(
                send_b.at[st, pl.ds(to * gp, gp)], got_b.at[st, k], sb.at[st, k], rb.at[st, k], inner[st](k)
            ))
    for copy in batch:
        copy.wait_recv()
    sends += batch
    for st in (0, 1):
        for q in range(gp):
            at = at_in[st] * gp + q
            total = (part[c * 8 + at] + got_a[at])[st * 32 : st * 32 + 32]
            for k in range(1, n):
                total = total + got_b[st, k, q].astype(F32)
            for i in range(4):
                for h in range(2):
                    send_c[st, q * 8 + i * 2 + h] = total[i * 8 : i * 8 + 8, h * 128 : h * 128 + 128]

    batch = []
    for k in range(1, n):
        for st in (0, 1):
            to = (at_out[st] + k) % n
            batch.append(remote(
                send_c.at[st, pl.ds(to * tp, tp)], got_c.at[st, k], sc.at[st, k], rc.at[st, k], outer[st](k)
            ))
    for copy in batch:
        copy.wait_recv()
    sends += batch
    for st in (0, 1):
        total = send_c[st, pl.ds(at_out[st] * tp, tp)]
        for k in range(1, n):
            total = total + got_c[st, k]
        got_d[g, st] = total

    batch = []
    for k in range(1, nx):
        batch.append(remote(got_d.at[g], got_d.at[g], sd.at[k], rd.at[k], along_x(k)))
    for copy in batch:
        copy.wait_recv()
    sends += batch
    for st in (0, 1):
        total = got_d[0, st]
        for k in range(1, nx):
            total = total + got_d[k, st]
        got_e[st, pl.ds(at_out[st] * tp, tp)] = total

    batch = []
    for k in range(1, n):
        for st in (0, 1):
            ref = got_e.at[st, pl.ds(at_out[st] * tp, tp)]
            batch.append(remote(ref, ref, se.at[st, k], re.at[st, k], outer[st](k)))
    for copy in batch:
        copy.wait_recv()
    sends += batch
    for st in (0, 1):
        for q in range(gp):
            lines = []
            for i in range(4):
                tiles = [got_e[st, q * 8 + i * 2 + h] for h in range(2)]
                lines.append(jnp.concatenate(tiles, axis=1))
            proj[c, st, at_in[st] * gp + q] = jnp.concatenate(lines, axis=0).astype(BF16)

    batch = []
    for k in range(1, n):
        for st in (0, 1):
            ref = proj.at[c, st, pl.ds(at_in[st] * gp, gp)]
            batch.append(remote(ref, ref, sf.at[st, k], rf.at[st, k], inner[st](k)))
    for copy in batch:
        copy.wait_recv()
    sends += batch

    copy = remote(proj.at[c], proj.at[c], sg, rg, sibling)
    sends.append(copy)

    def columns(core):
        total = jnp.zeros((64, 128), F32)
        for q in range(8):
            piece = jnp.concatenate([proj[core, 0, q], proj[core, 1, q]], axis=0)
            total = total + lax.dot_general(piece, panel[core * 8 + q], NT, preferred_element_type=F32)
        return total

    mine = columns(c)
    copy.wait_recv()
    got_h[g] = mine + columns(1 - c)

    batch = []
    for k in range(1, nx):
        batch.append(remote(got_h.at[g], got_h.at[g], sh.at[k], rh.at[k], along_x(k)))
    for copy in batch:
        copy.wait_recv()
    sends += batch
    rows = got_h[0]
    for k in range(1, nx):
        rows = rows + got_h[k]
    row_t[...] = rows

    gram = lax.dot_general(rows, rows, NT, precision=lax.Precision.HIGHEST, preferred_element_type=F32)
    gm[...] = jnp.concatenate([gram[0:32], gram[32:64]], axis=1)
    copy = remote(gm, got_i, si, ri, sibling)
    copy.wait_recv()
    sends.append(copy)
    got_j[z] = gm[...] + got_i[...]
    batch = []
    for k in range(1, n):
        batch.append(remote(got_j.at[z], got_j.at[z], sj.at[k], rj.at[k], along_z(k)))
    for copy in batch:
        copy.wait_recv()
    sends += batch
    total = got_j[0]
    for k in range(1, n):
        total = total + got_j[k]
    got_k[y] = total
    batch = []
    for k in range(1, n):
        batch.append(remote(got_k.at[y], got_k.at[y], sk.at[k], rk.at[k], along_y(k)))
    for copy in batch:
        copy.wait_recv()
    sends += batch
    total = got_k[0]
    for k in range(1, n):
        total = total + got_k[k]
    gram = jnp.concatenate([total[:, 0:64], total[:, 64:128]], axis=0)
    diagonal = lax.broadcasted_iota(jnp.int32, (64, 64), 0) == lax.broadcasted_iota(jnp.int32, (64, 64), 1)
    trace = jnp.sum(jnp.where(diagonal, gram, 0.0), axis=(0, 1), keepdims=True)
    gram_out[...] = gram * (64.0 / trace)
    rows_out[...] = row_t[...] * lax.rsqrt(trace / scale)
    for copy in sends:
        copy.wait_send()


def tail(n, nx, scale, panel, part):
    dma = pltpu.SemaphoreType.DMA
    vmem = pl.BlockSpec(memory_space=pltpu.VMEM)
    gp = 8 // n
    tp = 8 * gp // n
    sems = []
    for shape in ((), (2, n), (2, n), (nx,), (2, n), (2, n), (), (nx,), (), (n,), (n,)):
        sems += [dma(shape) if shape else dma] * 2
    return pl.pallas_call(
        functools.partial(tail_kernel, n, nx, scale),
        out_shape=(jax.ShapeDtypeStruct((64, 128), F32), jax.ShapeDtypeStruct((64, 64), F32)),
        in_specs=[vmem] * 2,
        out_specs=(vmem, vmem),
        scratch_shapes=[
            pltpu.VMEM((8, 64, 256), F32),
            pltpu.VMEM((2, 8, 32, 256), BF16),
            pltpu.VMEM((2, n, gp, 32, 256), BF16),
            pltpu.VMEM((2, n * tp, 8, 128), F32),
            pltpu.VMEM((2, n, tp, 8, 128), F32),
            pltpu.VMEM((nx, 2, tp, 8, 128), F32),
            pltpu.VMEM((2, n * tp, 8, 128), F32),
            pltpu.VMEM((2, 2, 8, 32, 256), BF16),
            pltpu.VMEM((64, 128), F32),
            pltpu.VMEM((nx, 64, 128), F32),
            pltpu.VMEM((32, 128), F32),
            pltpu.VMEM((32, 128), F32),
            pltpu.VMEM((32, 128), F32),
            pltpu.VMEM((n, 32, 128), F32),
            pltpu.VMEM((32, 128), F32),
            pltpu.VMEM((n, 32, 128), F32),
        ] + sems,
        compiler_params=pltpu.CompilerParams(collective_id=1, has_side_effects=True),
        name="tail",
    )(panel, part)


def body(n, nx, blocks, coords, counts, row_place, factor_one, factor_two, factor_three):
    slots = blocks.shape[0]
    live = (jnp.arange(slots) < counts[0]).astype(jnp.int32)
    places = look_place(coords.reshape(-1), row_place).reshape(3, slots)
    info = jnp.stack([places[1], places[2], places[0] % 2, live]).astype(jnp.int32)
    two = factor_two.reshape(2, 32, 2, 64).transpose(2, 1, 0, 3).reshape(64, 128)
    three = factor_three.reshape(2, 64, 64).transpose(1, 0, 2).reshape(64, 128)
    one = factor_one.reshape(2, 32, 2, 64).transpose(3, 2, 0, 1).reshape(64, 128)
    all2, all3 = gather_factors(n, two, three)
    panel, part = local_terms(
        info, blocks, all2.reshape(-1, 64, 128), all3.reshape(-1, 64, 128), one
    )
    scale = 2.0 * 64 * 64 * 2 * n * n
    rows, gram = tail(n, nx, scale, panel, part)
    new_rows = rows.reshape(64, 2, 2, 32).transpose(2, 3, 1, 0).reshape(2, 4096)
    return (new_rows, gram)


def solution(mesh):
    n = math.isqrt(mesh.shape["dev"] // 2)
    nx = mesh.shape["grp"]
    placed = (
        P(("grp", "dev"), None, None),
        P(None, ("grp", "dev")),
        P(("grp", "dev")),
        P(),
        P("dev", None),
        P("dev", None),
        P("dev", None),
    )
    return jax.shard_map(
        functools.partial(body, n, nx), mesh=mesh, in_specs=placed, out_specs=(P("dev", None), P()), check_vma=False
    )
```

time: 1270 us -> 122 us (0.10)
  the two profiles are of different devices: /device:TPU:4 before, /device:TPU:16 now
where the time goes in v1:
time: 122 us; the launch traced here: 121 us
  Pallas kernels  110 us (90%)
  local copies, waits for them, and re-layouts  8.37 us (7%)
  other arithmetic  1.53 us (1%)
  between operations  1.34 us (1%)
    pallas_call x1, Pallas kernels, tail(): pl.pallas_call(functools.partial(tail_kernel, n, nx, scale), out_shape=(j...  55.4 us
    pallas_call x1, Pallas kernels, gather_factors(): pl.pallas_call(functools.partial(gather_kernel, n), out_shape=(shape, sha...  41 us
    pallas_call x1, Pallas kernels, local_terms(): pl.pallas_call(local_kernel, grid_spec=pltpu.PrefetchScalarGridSpec(num_s...  13.8 us

profile of v1, /device:TPU:16, one launch (start us, length us, event | category | flops | bytes accessed | tf_op | source)
XLA Modules:
  0.0 121.5 jit_solution(2575512795967338137)
XLA Ops:
  1.3 0.8 eq.17
  2.1 0.9 select_reduce_fusion
  2.9 0.1 slice_bitcast_fusion.1
  3.0 0.6 pad_add_fusion.info
  3.6 0.8 reshape.69
  4.4 0.7 copy.27.f1
  5.1 0.8 reshape.63
  6.0 0.7 reshape.64.two
  6.7 0.8 reshape.65
  7.5 0.7 reshape.66.three
  8.2 41.0 %gather_factors.1 = (bf16[8,8,2,64,128]{4,3,2,1,0:T(8,128)(2,1)}, bf16[8,8,2,64,128]{4,3,2,1,0:T(8,128)(2,1)}) custom-call(bf16[64,128]{1,0:T(8,128)(2,1)} %reshape.64.two, bf16[64,128]{1,0:T(8,128)(2,1)} %reshape.66.three), custom_call_target="tpu_custom_call" | custom-call | tf_op jit(solution)/shard_map/gather_factors/pallas_call | solution.py:119
  49.2 13.8 %local_terms.1 = (bf16[16,128,256]{2,1,0:T(8,128)(2,1)}, f32[16,64,256]{2,1,0:T(8,128)}) custom-call(s32[4,8]{1,0:T(4,128)} %pad_add_fusion.info, bf16[8,64,4096]{2,1,0:T(8,128)(2,1)} %blk.1, bf16[128,64,128]{2,1,0:T(8,128)(2,1)} %bitcast.22, bf16[128,64,128]{2,1,0:T(8,128)(2,1)} %bitcast.23, bf16[64,128]{1,0:T(8,128)(2,1)} %copy.27.f1), custom_call_target="tpu_custom_call" | custom-call | tf_op jit(solution)/shard_map/local_terms/pallas_call | solution.py:208
  63.0 55.4 %tail.1 = (f32[64,128]{1,0:T(8,128)}, f32[64,64]{1,0:T(8,128)}) custom-call(bf16[16,128,256]{2,1,0:T(8,128)(2,1)} %get-tuple-element.10.panel, f32[16,64,256]{2,1,0:T(8,128)} %get-tuple-element.11.part), custom_call_target="tpu_custom_call" | custom-call | tf_op jit(solution)/shard_map/tail/pallas_call | solution.py:422
  118.5 0.8 copy.28
  119.3 0.1 copy.29
  119.4 0.7 reshape.72
  120.1 1.4 %copy.36 = f32[64,64]{1,0:T(8,128)} copy(f32[64,64]{1,0:T(8,128)} %get-tuple-element.20) | data formatting | bytes 32768
  (4 shorter events, 0.1 us)
